TPU v7x, 32 devices: a whole 2x2x4 slice. The times are simulated.
32 devices in a mesh: own: 8 (over z, core), help: 4 (over y, x).
Axes of the slice: x: 2, y: 2, z: 4, core: 2. Of those that a mesh axis runs over, the one named last changes fastest.
Arguments:
- records: bfloat16 [16384, 256], P(('own', 'help')), may hold values from -6 to 6
- owner: int32 [16384, 1], P(('own', 'help')), may hold values from 0 to 7; in each aligned block of 512 rows (0 to 511, 512 to 1023, ...) at most 128 rows name the same one
- subkey: int32 [16384], P(('own', 'help')), may hold values from 0 to 3
- source: int32 [16384], P(('own', 'help')), may hold values from 0 to 3
Outputs:
- resolved: bfloat16 [16384, 256], P(('own', 'help'))
Inputs may be any that keep to these rules, and one draw needn't show every extreme that they name: Among the 512 records of one device (aligned blocks of rows), no owner is named more than 128 times, and in every draw some device names some owner exactly 128 times.
All inputs are finite; a program needn't handle non-finite values.
Results may differ from a plain program's by a relative error of at most 0.0052.
Values may be sent and summed in bfloat16 or wider, within the bound.
No kernel may reach another device: no remote copies, remote signals or barrier semaphores. Data moves between devices by JAX's collectives and lax.ppermute only.
A program may use at most 192 MiB of HBM per device.

v0:
```python
import jax
import jax.numpy as jnp
from jax import lax
from jax.sharding import PartitionSpec as P

SOURCES = 4
epsilon = 1e-06
sharpness = 4.0


def normalized(records):
    values_f = records.astype(jnp.float32)
    inverse = lax.rsqrt(jnp.mean(values_f * values_f, axis=1, keepdims=True) + epsilon)
    return (values_f * inverse).astype(jnp.bfloat16)


def pair_weights(query_rows, query_codes, key_rows, key_codes):
    scores = lax.dot_general(
        query_rows, key_rows, (((1,), (1,)), ((), ())), preferred_element_type=jnp.float32
    )
    matched = (query_codes[:, None] >= 0) & (key_codes[None, :] >= 0)
    matched = matched & (query_codes[:, None] // SOURCES == key_codes[None, :] // SOURCES)
    matched = matched & (query_codes[:, None] % SOURCES != key_codes[None, :] % SOURCES)
    return jnp.where(
        matched, jnp.exp(scores * (sharpness / query_rows.shape[1])), jnp.zeros_like(scores)
    )


def resolve(held_rows, partner, mass):
    merged = held_rows.astype(jnp.float32) + partner * lax.rsqrt(1.0 + mass)[:, None]
    return merged.astype(jnp.bfloat16)


def shards(records, owner, subkey, source):
    row_count = records.shape[0]
    width = records.shape[1]
    owners = lax.axis_size("own")
    slot_count = 2 * row_count
    capacity = slot_count // owners
    scaled = normalized(records)
    target = owner[:, 0]
    onehot = (target[:, None] == jnp.arange(owners, dtype=jnp.int32)[None, :]).astype(jnp.int32)
    slot_rank = jnp.sum(jnp.cumsum(onehot, axis=0) * onehot, axis=1) - 1
    slot_index = target * capacity + slot_rank
    outbox = jnp.zeros((slot_count, width), jnp.bfloat16).at[slot_index].set(scaled)
    out_codes = jnp.full((slot_count,), -1, jnp.int32).at[slot_index].set(subkey * SOURCES + source)
    inbox, in_codes = (
        lax.all_to_all(
            outbox.reshape(owners, capacity, width), "own", split_axis=0, concat_axis=0, tiled=True
        ),
        lax.all_to_all(
            out_codes.reshape(owners, capacity), "own", split_axis=0, concat_axis=0, tiled=True
        ),
    )
    held_rows = inbox.reshape(slot_count, width)
    held_codes = in_codes.reshape(slot_count)
    incoming = (
        lax.all_gather(held_rows, "help", axis=0, tiled=True),
        lax.all_gather(held_codes, "help", axis=0, tiled=True),
    )
    weight = pair_weights(held_rows, held_codes, incoming[0], incoming[1])
    partner_next = jnp.dot(
        weight.astype(jnp.bfloat16), incoming[0], preferred_element_type=jnp.float32
    )
    mass = jnp.sum(weight, axis=1)
    merged = resolve(held_rows, partner_next, mass).reshape(owners, capacity, width)
    returned = lax.all_to_all(merged, "own", split_axis=0, concat_axis=0, tiled=True).reshape(
        slot_count, width
    )
    return returned[slot_index]


def solution(mesh):
    return jax.shard_map(
        shards,
        mesh=mesh,
        in_specs=(
            P(("own", "help"), None),
            P(("own", "help"), None),
            P(("own", "help")),
            P(("own", "help")),
        ),
        out_specs=P(("own", "help"), None),
        check_vma=False,
    )
```

profile of v0, /device:TPU:0, one launch (start us, length us, event | category | flops | bytes accessed | tf_op | source)
XLA Modules:
  0.0 117.5 jit_solution(4763169931657767500)
XLA Ops:
  6.5 0.0 all-gather.2.cloned.1.call-start
  6.5 0.7 fusion.20
  7.2 1.1 reduce-window.6
  8.4 0.2 slice_reduce_fusion
  8.6 0.8 fusion.19
  9.4 0.7 compare_select_fusion
  10.1 1.1 fusion.13
  11.2 3.0 %scatter_custom_fusion = bf16[1024,256]{1,0:T(8,128)(2,1)S(1)} fusion(s32[512]{0:T(512)S(1)} %bitcast.30, bf16[512,256]{1,0:T(8,128)(2,1)} %param.4, f32[512]{0:T(512)S(1)} %add_rsqrt_fusion.1, bf16[]{:T(256)} %constant.61.clone.1), kind=kCustom, calls=%fused_computation.14 | custom fusion | flops 393216 | bytes 788482 | tf_op jit(solution)/shard_map/scatter | solution.py:45
  14.2 21.6 %all_to_all.19 = bf16[8,128,256]{2,1,0:T(8,128)(2,1)} all-to-all(bf16[8,128,256]{2,1,0:T(8,128)(2,1)S(1)} %bitcast.23), channel_id=1, replica_groups=mesh['own'=8,'help'=4] {'own'}, dimensions={0} | all-to-all | bytes 1048576 | tf_op jit(solution)/shard_map/all_to_all | solution.py:48
  35.8 0.0 all-gather.2.cloned.1.call-update
  35.8 0.7 multiply_add_fusion
  36.5 2.4 %scatter_custom_fusion.1 = s32[1024]{0:T(1024)S(1)} fusion(s32[512]{0:T(512)S(1)} %bitcast.31, s32[512]{0:T(512)S(1)} %multiply_add_fusion, s32[]{:T(128)} %constant.64.clone.1), kind=kCustom, calls=%fused_computation.45 | custom fusion | bytes 4100 | tf_op jit(solution)/shard_map/scatter | solution.py:46
  38.9 7.9 %all_to_all.20 = s32[8,1,128]{2,1,0:T(1,128)S(1)} all-to-all(s32[8,1,128]{2,1,0:T(1,128)S(1)} %bitcast.29), channel_id=1, replica_groups=mesh['own'=8,'help'=4] {'own'}, dimensions={0} | all-to-all | bytes 8192 | tf_op jit(solution)/shard_map/all_to_all | solution.py:51
  46.9 8.3 %all_gather.6 = s32[4096]{0:T(1024)S(1)} all-gather(s32[1024]{0:T(1024)S(1)} %bitcast.24), channel_id=1, replica_groups=mesh['own'=8,'help'=4] {'help'}, dimensions={0}, use_global_device_ids=true | all-gather | bytes 20480 | tf_op jit(solution)/shard_map/all_gather | solution.py:59
  55.3 15.0 %all-gather.2.cloned.1.call-done = bf16[4096,256]{1,0:T(8,128)(2,1)} async-done(((bf16[1024,256]{1,0:T(8,128)(2,1)}), bf16[4096,256]{1,0:T(8,128)(2,1)}) %all-gather.2.cloned.1.call-update) | async-done | bytes 2097168 | tf_op jit(solution)/shard_map/all_gather | solution.py:58
  70.3 0.0 copy-start
  70.3 0.0 copy-start.1
  70.3 9.7 %fusion = (f32[1024]{0:T(1024)S(1)}, f32[1024,4096]{1,0:T(8,128)S(1)}) fusion(s32[4096]{0:T(1024)S(1)} %get-tuple-element.6, s32[4096]{0:T(1024)S(1)} %get-tuple-element.5, s32[1024]{0:T(1024)S(1)} %get-tuple-element.8, s32[1024]{0:T(1024)S(1)} %get-tuple-element.7, pred[4096]{0:T(1024)(128)(4,1)S(1)} %broadcast_compare_fusion, ...), kind=kOutput, calls=%fused_computation.4 | convolution fusion | flops 2181037056 | bytes 19448832 | tf_op jit(solution)/shard_map/dot_general | solution.py:18
  80.0 0.0 copy-done
  80.0 0.0 copy-done.1
  80.0 8.1 %fusion.10 = bf16[1024,256]{1,0:T(8,128)(2,1)} fusion(bf16[4096,256]{1,0:T(8,128)(2,1)S(1)} %copy-done.1, f32[1024,4096]{1,0:T(8,128)S(1)} %get-tuple-element.10, s32[4096]{0:T(1024)S(1)} %get-tuple-element.6, s32[4096]{0:T(1024)S(1)} %get-tuple-element.5, s32[1024]{0:T(1024)S(1)} %get-tuple-element.8, s32[1024]{0:T(1024)S(1)} %get-tuple-element.7, ...), kind=kOutput, calls=%fused_computation.9 | convolution fusion | flops 2182086656 | bytes 19973120 | tf_op jit(solution)/shard_map/dot_general | solution.py:62
  88.2 4.6 %all-to-all-start.2 = ((bf16[8,128,256]{2,1,0:T(8,128)(2,1)}), bf16[8,128,256]{2,1,0:T(8,128)(2,1)S(1)}, u32[]{:S(2)}, u32[]{:S(2)}) async-start(bf16[8,128,256]{2,1,0:T(8,128)(2,1)} %bitcast.10), calls=%async_computation.2 | async-start | bytes 1048576 | tf_op jit(solution)/shard_map/all_to_all | solution.py:67
  92.8 15.4 %all-to-all-done.2 = bf16[8,128,256]{2,1,0:T(8,128)(2,1)S(1)} async-done(((bf16[8,128,256]{2,1,0:T(8,128)(2,1)}), bf16[8,128,256]{2,1,0:T(8,128)(2,1)S(1)}, u32[]{:S(2)}, u32[]{:S(2)}) %all-to-all-start.2) | async-done | bytes 524320 | tf_op jit(solution)/shard_map/all_to_all | solution.py:67
  108.1 2.6 %gather_fusion = bf16[512,256]{1,0:T(8,128)(2,1)} fusion(bf16[1024,256]{1,0:T(8,128)(2,1)S(1)} %bitcast.19, s32[1024]{0:T(1024)S(1)} %pad_clamp_fusion), kind=kCustom, calls=%fused_computation | custom fusion | bytes 526336 | tf_op jit(solution)/shard_map/gather | solution.py:70
  (10 shorter events, 0.1 us)
Async XLA Ops:
  6.5 63.7 %all-gather.2.cloned.1.call-start = ((), (), s32[]{:S(2)}) async-start(), calls=%async_computation.3 | async-start | bytes 2621440 | tf_op jit(solution)/shard_map/all_gather | solution.py:58
  70.3 9.7 %copy-start = (bf16[8,128,256]{2,1,0:T(8,128)(2,1)S(1)}, bf16[8,128,256]{2,1,0:T(8,128)(2,1)}, u32[]{:S(2)}) copy-start(bf16[8,128,256]{2,1,0:T(8,128)(2,1)} %all_to_all.19) | copy-start | bytes 1572868
  70.3 9.7 %copy-start.1 = (bf16[4096,256]{1,0:T(8,128)(2,1)S(1)}, bf16[4096,256]{1,0:T(8,128)(2,1)}, u32[]{:S(2)}) copy-start(bf16[4096,256]{1,0:T(8,128)(2,1)} %all-gather.2.cloned.1.call-done) | copy-start | bytes 6291460
  88.2 20.0 %all-to-all-start.2 = ((bf16[8,128,256]{2,1,0:T(8,128)(2,1)}), bf16[8,128,256]{2,1,0:T(8,128)(2,1)S(1)}, u32[]{:S(2)}, u32[]{:S(2)}) async-start(bf16[8,128,256]{2,1,0:T(8,128)(2,1)} %bitcast.10), calls=%async_computation.2 | async-start | bytes 1048576 | tf_op jit(solution)/shard_map/all_to_all | solution.py:67
Sparse Core Ops, SparseCore 0:
  35.9 34.2 all-gather.1
where the time goes:
time: 118 us
  blocking collectives  37.8 us (32%)
  waiting for transfers between devices  30.4 us (26%)
  matrix products  17.9 us (15%)
  between operations  13.5 us (11%)
  other arithmetic  8.15 us (7%)
  local copies, waits for them, and re-layouts  5.24 us (4%)
  starting transfers between devices  4.61 us (4%)
    all_to_all x1, blocking collectives, shards(): lax.all_to_all(outbox.reshape(owners, capacity, width), 'own', split_axis...  21.6 us
    all_to_all x1, waiting for transfers between devices, shards(): lax.all_to_all(merged, 'own', split_axis=0, concat_axis=0, tiled=True)  15.4 us
    all_gather x1, waiting for transfers between devices, shards(): lax.all_gather(held_rows, 'help', axis=0, tiled=True)  15 us
    dot_general x1, matrix products, pair_weights(): lax.dot_general(query_rows, key_rows, (((1,), (1,)), ((), ())), preferred...  9.72 us
    all_gather x1, blocking collectives, shards(): lax.all_gather(held_codes, 'help', axis=0, tiled=True)  8.34 us
    dot_general x1, matrix products, shards(): jnp.dot(weight.astype(jnp.bfloat16), incoming[0], preferred_element_type=...  8.14 us
    all_to_all x1, blocking collectives, shards(): lax.all_to_all(out_codes.reshape(owners, capacity), 'own', split_axis=0,...  7.92 us
    all_to_all x1, starting transfers between devices, shards(): lax.all_to_all(merged, 'own', split_axis=0, concat_axis=0, tiled=True)  4.61 us
  transfers between devices with their start and end apart: 2, of which 2 were waited for; matrix products, arithmetic and copies ran while one was open for 3% of the time, Pallas kernels for 0%

commit v1 on v0

--- a/solution.py
+++ b/solution.py
@@ -6,6 +6,29 @@
 SOURCES = 4
 epsilon = 1e-06
 sharpness = 4.0
+
+
+def cut_along(array, dim, size):
+    dims = array.shape
+    blocks = array.reshape(*dims[:dim], size, dims[dim] // size, *dims[dim + 1 :])
+    return jnp.moveaxis(blocks, dim, 0)
+
+
+def joined_along(tiles, dim):
+    dims = list(tiles.shape[1:])
+    dims[dim] *= tiles.shape[0]
+    return jnp.moveaxis(tiles, 0, dim).reshape(dims)
+
+
+def pairwise_exchange(array, axis, split_dim, concat_dim):
+    peers, index = (lax.axis_size(axis), lax.axis_index(axis))
+    blocks = cut_along(array, split_dim, peers)
+    done = [blocks[index]]
+    for lap in range(1, peers):
+        sent = blocks[index ^ lap]
+        done.append(lax.ppermute(sent, axis, [(i, i ^ lap) for i in range(peers)]))
+    blocks = jnp.stack(done)[index ^ jnp.arange(peers)]
+    return joined_along(blocks, concat_dim)
 
 
 def normalized(records):
@@ -64,9 +87,7 @@
     )
     mass = jnp.sum(weight, axis=1)
     merged = resolve(held_rows, partner_next, mass).reshape(owners, capacity, width)
-    returned = lax.all_to_all(merged, "own", split_axis=0, concat_axis=0, tiled=True).reshape(
-        slot_count, width
-    )
+    returned = pairwise_exchange(merged, "own", 0, 0).reshape(slot_count, width)
     return returned[slot_index]
 
 

time: 118 us -> 113 us (0.958)
  blocking collectives: 37.8 us -> 29.9 us
  starting transfers between devices: 4.61 us -> 11.5 us
  waiting for transfers between devices: 30.4 us -> 25.6 us
  local copies, waits for them, and re-layouts: 5.24 us -> 6.49 us
    all_to_all x1, waiting for transfers between devices: 15.4 us -> 5.34 us  [shards(): lax.all_to_all(out_codes.reshape(owners, capacity), 'own', split_axis=0,...]
    ppermute x0 -> x7, starting transfers between devices: none -> 8.18 us  [pairwise_exchange(): done.append(lax.ppermute(sent, axis, [(i, i ^ lap) for i in range(peers)]))]
    all_to_all x1 -> x0, blocking collectives: 7.92 us -> none  [shards(): lax.all_to_all(out_codes.reshape(owners, capacity), 'own', split_axis=0,...]
    ppermute x0 -> x7, waiting for transfers between devices: none -> 6.62 us  [pairwise_exchange(): done.append(lax.ppermute(sent, axis, [(i, i ^ lap) for i in range(peers)]))]
    all_gather x1, waiting for transfers between devices: 15 us -> 13.6 us  [shards(): lax.all_gather(held_rows, 'help', axis=0, tiled=True)]
    all_to_all x1, starting transfers between devices: 4.61 us -> 3.31 us  [shards(): lax.all_to_all(out_codes.reshape(owners, capacity), 'own', split_axis=0,...]
  transfers between devices with their start and end apart: 2 -> 9, of which waited for: 2 -> 3; matrix products, arithmetic and copies ran while one was open for 3% -> 3% of each run, Pallas kernels for 0% -> 0%
where the time goes in v1:
time: 113 us; the launch traced here: 112 us
  blocking collectives  29.9 us (26%)
  waiting for transfers between devices  25.6 us (23%)
  matrix products  17 us (15%)
  between operations  13.6 us (12%)
  starting transfers between devices  11.5 us (10%)
  other arithmetic  8.17 us (7%)
  local copies, waits for them, and re-layouts  6.49 us (6%)
    all_to_all x1, blocking collectives, shards(): lax.all_to_all(outbox.reshape(owners, capacity, width), 'own', split_axis...  21.6 us
    all_gather x1, waiting for transfers between devices, shards(): lax.all_gather(held_rows, 'help', axis=0, tiled=True)  13.6 us
    dot_general x1, matrix products, pair_weights(): lax.dot_general(query_rows, key_rows, (((1,), (1,)), ((), ())), preferred...  9.72 us
    all_gather x1, blocking collectives, shards(): lax.all_gather(held_codes, 'help', axis=0, tiled=True)  8.34 us
    ppermute x7, starting transfers between devices, pairwise_exchange(): done.append(lax.ppermute(sent, axis, [(i, i ^ lap) for i in range(peers)]))  8.18 us
    dot_general x1, matrix products, shards(): jnp.dot(weight.astype(jnp.bfloat16), incoming[0], preferred_element_type=...  7.27 us
    ppermute x7, waiting for transfers between devices, pairwise_exchange(): done.append(lax.ppermute(sent, axis, [(i, i ^ lap) for i in range(peers)]))  6.62 us
    all_to_all x1, waiting for transfers between devices, shards(): lax.all_to_all(out_codes.reshape(owners, capacity), 'own', split_axis=0,...  5.34 us
  transfers between devices with their start and end apart: 9, of which 3 were waited for; matrix products, arithmetic and copies ran while one was open for 3% of the time, Pallas kernels for 0%

profile of v1, /device:TPU:0, one launch (start us, length us, event | category | flops | bytes accessed | tf_op | source)
XLA Modules:
  0.0 112.3 jit_solution(1630167143927092335)
XLA Ops:
  6.5 0.0 all-gather.2.cloned.1.call-start
  6.5 0.7 fusion.20
  7.2 1.1 %reduce-window.6 = s32[8,4,128]{2,0,1:T(8,128)S(1)} reduce-window(s32[8,4,128]{2,0,1:T(8,128)S(1)} %fusion.20, s32[]{:T(128)} %constant.45.clone.1), window={size=1x1x128 pad=0_0x0_0x127_0}, to_apply=%region_0.0 | reduce-window | flops 520192 | bytes 32772 | tf_op jit(solution)/shard_map/reduce-window
  8.4 0.2 slice_reduce_fusion
  8.6 0.8 fusion.19
  9.4 0.7 compare_select_fusion
  10.1 1.1 fusion.13
  11.2 3.0 %scatter_custom_fusion = bf16[1024,256]{1,0:T(8,128)(2,1)S(1)} fusion(s32[512]{0:T(512)S(1)} %bitcast.62, bf16[512,256]{1,0:T(8,128)(2,1)} %param.4, f32[512]{0:T(512)S(1)} %add_rsqrt_fusion.1, bf16[]{:T(256)} %constant.40.clone.1), kind=kCustom, calls=%fused_computation.15 | custom fusion | flops 393216 | bytes 788482 | tf_op jit(solution)/shard_map/scatter | solution.py:68
  14.2 21.6 %all_to_all.14 = bf16[8,128,256]{2,1,0:T(8,128)(2,1)} all-to-all(bf16[8,128,256]{2,1,0:T(8,128)(2,1)S(1)} %bitcast.54), channel_id=1, replica_groups=mesh['own'=8,'help'=4] {'own'}, dimensions={0} | all-to-all | bytes 1048576 | tf_op jit(solution)/shard_map/all_to_all | solution.py:71
  35.8 0.0 all-gather.2.cloned.1.call-update
  35.8 0.7 multiply_add_fusion
  36.5 3.0 %scatter_custom_fusion.1 = s32[1024]{0:T(1024)} fusion(s32[512]{0:T(512)S(1)} %bitcast.63, s32[512]{0:T(512)S(1)} %multiply_add_fusion, s32[]{:T(128)} %constant.46.clone.1), kind=kCustom, calls=%fused_computation.63 | custom fusion | bytes 4100 | tf_op jit(solution)/shard_map/scatter | solution.py:69
  39.5 3.3 %all-to-all-start.1 = ((s32[8,1,128]{2,1,0:T(1,128)}), s32[8,1,128]{2,1,0:T(1,128)S(1)}, u32[]{:S(2)}, u32[]{:S(2)}) async-start(s32[8,1,128]{2,1,0:T(1,128)} %bitcast.8), calls=%async_computation.1 | async-start | bytes 8192 | tf_op jit(solution)/shard_map/all_to_all | solution.py:74
  42.9 5.3 %all-to-all-done.1 = s32[8,1,128]{2,1,0:T(1,128)S(1)} async-done(((s32[8,1,128]{2,1,0:T(1,128)}), s32[8,1,128]{2,1,0:T(1,128)S(1)}, u32[]{:S(2)}, u32[]{:S(2)}) %all-to-all-start.1) | async-done | bytes 4128 | tf_op jit(solution)/shard_map/all_to_all | solution.py:74
  48.2 8.3 %all_gather.6 = s32[4096]{0:T(1024)S(1)} all-gather(s32[1024]{0:T(1024)S(1)} %bitcast.57), channel_id=1, replica_groups=mesh['own'=8,'help'=4] {'help'}, dimensions={0}, use_global_device_ids=true | all-gather | bytes 20480 | tf_op jit(solution)/shard_map/all_gather | solution.py:82
  56.6 13.6 %all-gather.2.cloned.1.call-done = bf16[4096,256]{1,0:T(8,128)(2,1)} async-done(((bf16[1024,256]{1,0:T(8,128)(2,1)}), bf16[4096,256]{1,0:T(8,128)(2,1)}) %all-gather.2.cloned.1.call-update) | async-done | bytes 2097168 | tf_op jit(solution)/shard_map/all_gather | solution.py:81
  70.3 0.0 copy-start
  70.3 0.0 copy-start.1
  70.3 9.7 %fusion = (f32[1024]{0:T(1024)S(1)}, f32[1024,4096]{1,0:T(8,128)S(1)}) fusion(s32[4096]{0:T(1024)S(1)} %get-tuple-element.14, s32[4096]{0:T(1024)S(1)} %get-tuple-element.13, s32[1024]{0:T(1024)S(1)} %get-tuple-element.16, s32[1024]{0:T(1024)S(1)} %get-tuple-element.15, pred[4096]{0:T(1024)(128)(4,1)S(1)} %broadcast_compare_fusion, ...), kind=kOutput, calls=%fused_computation.5 | convolution fusion | flops 2181037056 | bytes 19448832 | tf_op jit(solution)/shard_map/dot_general | solution.py:41
  80.0 0.0 copy-done
  80.0 0.0 copy-done.1
  80.0 7.3 %fusion.10 = bf16[1024,256]{1,0:T(8,128)(2,1)S(1)} fusion(bf16[4096,256]{1,0:T(8,128)(2,1)S(1)} %copy-done.1, f32[1024,4096]{1,0:T(8,128)S(1)} %get-tuple-element.18, s32[4096]{0:T(1024)S(1)} %get-tuple-element.14, s32[4096]{0:T(1024)S(1)} %get-tuple-element.13, s32[1024]{0:T(1024)S(1)} %get-tuple-element.16, s32[1024]{0:T(1024)S(1)} %get-tuple-element.15, ...), kind=kOutput, calls=%fused_computation.10 | convolution fusion | flops 2182086656 | bytes 19973120 | tf_op jit(solution)/shard_map/dot_general | solution.py:85
  87.3 0.1 dynamic-slice_bitcast_fusion
  87.4 0.1 collective-permute-start
  87.5 1.6 %collective-permute-start.1 = (bf16[1,128,256]{2,1,0:T(8,128)(2,1)S(1)}, bf16[1,128,256]{2,1,0:T(8,128)(2,1)S(1)}, u32[]{:S(2)}, u32[]{:S(2)}) collective-permute-start(bf16[1,128,256]{2,1,0:T(8,128)(2,1)S(1)} %get-tuple-element.10), channel_id=1, source_target_pairs={{0,8},{4,12},{8,0},{12,4},{16,24},{20,28},{24,16},{28,20},{1,9},{5... | collective-permute-start | bytes 196616 | tf_op jit(solution)/shard_map/ppermute | solution.py:29
  89.0 0.3 collective-permute-start.2
  89.3 2.4 %collective-permute-start.3 = (bf16[1,128,256]{2,1,0:T(8,128)(2,1)S(1)}, bf16[1,128,256]{2,1,0:T(8,128)(2,1)S(1)}, u32[]{:S(2)}, u32[]{:S(2)}) collective-permute-start(bf16[1,128,256]{2,1,0:T(8,128)(2,1)S(1)} %get-tuple-element.8), channel_id=1, source_target_pairs={{0,16},{4,20},{8,24},{12,28},{16,0},{20,4},{24,8},{28,12},{1,17},{... | collective-permute-start | bytes 196616 | tf_op jit(solution)/shard_map/ppermute | solution.py:29
  91.7 0.2 collective-permute-start.4
  91.9 0.0 collective-permute-done
  91.9 3.3 %collective-permute-start.5 = (bf16[1,128,256]{2,1,0:T(8,128)(2,1)S(1)}, bf16[1,128,256]{2,1,0:T(8,128)(2,1)S(1)}, u32[]{:S(2)}, u32[]{:S(2)}) collective-permute-start(bf16[1,128,256]{2,1,0:T(8,128)(2,1)S(1)} %get-tuple-element.6), channel_id=1, source_target_pairs={{0,24},{4,28},{8,16},{12,20},{16,8},{20,12},{24,0},{28,4},{1,25},{... | collective-permute-start | bytes 196616 | tf_op jit(solution)/shard_map/ppermute | solution.py:29
  95.2 0.0 collective-permute-done.1
  95.3 0.3 collective-permute-start.6
  95.6 0.0 collective-permute-done.2
  95.6 0.0 collective-permute-done.3
  95.6 6.6 %collective-permute-done.4 = bf16[1,128,256]{2,1,0:T(8,128)(2,1)S(1)} collective-permute-done((bf16[1,128,256]{2,1,0:T(8,128)(2,1)S(1)}, bf16[1,128,256]{2,1,0:T(8,128)(2,1)S(1)}, u32[]{:S(2)}, u32[]{:S(2)}) %collective-permute-start.4) | collective-permute-done | bytes 65568 | tf_op jit(solution)/shard_map/ppermute | solution.py:29
  102.2 0.0 collective-permute-done.5
  102.3 0.0 collective-permute-done.6
  102.3 0.6 gather_fusion
  102.9 2.6 %gather_fusion.1 = bf16[512,256]{1,0:T(8,128)(2,1)} fusion(bf16[1024,256]{1,0:T(8,128)(2,1)S(1)} %bitcast.50, s32[1024]{0:T(1024)S(1)} %pad_clamp_fusion), kind=kCustom, calls=%fused_computation.1 | custom fusion | bytes 526336 | tf_op jit(solution)/shard_map/gather | solution.py:91
  (19 shorter events, 0.2 us)
Async XLA Ops:
  6.5 63.7 %all-gather.2.cloned.1.call-start = ((), (), s32[]{:S(2)}) async-start(), calls=%async_computation.2 | async-start | bytes 2621440 | tf_op jit(solution)/shard_map/all_gather | solution.py:81
  39.5 8.7 %all-to-all-start.1 = ((s32[8,1,128]{2,1,0:T(1,128)}), s32[8,1,128]{2,1,0:T(1,128)S(1)}, u32[]{:S(2)}, u32[]{:S(2)}) async-start(s32[8,1,128]{2,1,0:T(1,128)} %bitcast.8), calls=%async_computation.1 | async-start | bytes 8192 | tf_op jit(solution)/shard_map/all_to_all | solution.py:74
  70.3 9.7 %copy-start = (bf16[8,128,256]{2,1,0:T(8,128)(2,1)S(1)}, bf16[8,128,256]{2,1,0:T(8,128)(2,1)}, u32[]{:S(2)}) copy-start(bf16[8,128,256]{2,1,0:T(8,128)(2,1)} %all_to_all.14) | copy-start | bytes 1572868
  70.3 9.7 %copy-start.1 = (bf16[4096,256]{1,0:T(8,128)(2,1)S(1)}, bf16[4096,256]{1,0:T(8,128)(2,1)}, u32[]{:S(2)}) copy-start(bf16[4096,256]{1,0:T(8,128)(2,1)} %all-gather.2.cloned.1.call-done) | copy-start | bytes 6291460
  87.4 4.6 %collective-permute-start = (bf16[1,128,256]{2,1,0:T(8,128)(2,1)S(1)}, bf16[1,128,256]{2,1,0:T(8,128)(2,1)S(1)}, u32[]{:S(2)}, u32[]{:S(2)}) collective-permute-start(bf16[1,128,256]{2,1,0:T(8,128)(2,1)S(1)} %get-tuple-element.11), channel_id=1, source_target_pairs={{0,4},{4,0},{8,12},{12,8},{16,20},{20,16},{24,28},{28,24},{1,5},{5... | collective-permute-start | bytes 196616 | tf_op jit(solution)/shard_map/ppermute | solution.py:29
  87.5 7.8 %collective-permute-start.1 = (bf16[1,128,256]{2,1,0:T(8,128)(2,1)S(1)}, bf16[1,128,256]{2,1,0:T(8,128)(2,1)S(1)}, u32[]{:S(2)}, u32[]{:S(2)}) collective-permute-start(bf16[1,128,256]{2,1,0:T(8,128)(2,1)S(1)} %get-tuple-element.10), channel_id=1, source_target_pairs={{0,8},{4,12},{8,0},{12,4},{16,24},{20,28},{24,16},{28,20},{1,9},{5... | collective-permute-start | bytes 196616 | tf_op jit(solution)/shard_map/ppermute | solution.py:29
  89.0 6.6 %collective-permute-start.2 = (bf16[1,128,256]{2,1,0:T(8,128)(2,1)S(1)}, bf16[1,128,256]{2,1,0:T(8,128)(2,1)S(1)}, u32[]{:S(2)}, u32[]{:S(2)}) collective-permute-start(bf16[1,128,256]{2,1,0:T(8,128)(2,1)S(1)} %get-tuple-element.9), channel_id=1, source_target_pairs={{0,12},{4,8},{8,4},{12,0},{16,28},{20,24},{24,20},{28,16},{1,13},{... | collective-permute-start | bytes 196616 | tf_op jit(solution)/shard_map/ppermute | solution.py:29
  89.3 6.3 %collective-permute-start.3 = (bf16[1,128,256]{2,1,0:T(8,128)(2,1)S(1)}, bf16[1,128,256]{2,1,0:T(8,128)(2,1)S(1)}, u32[]{:S(2)}, u32[]{:S(2)}) collective-permute-start(bf16[1,128,256]{2,1,0:T(8,128)(2,1)S(1)} %get-tuple-element.8), channel_id=1, source_target_pairs={{0,16},{4,20},{8,24},{12,28},{16,0},{20,4},{24,8},{28,12},{1,17},{... | collective-permute-start | bytes 196616 | tf_op jit(solution)/shard_map/ppermute | solution.py:29
  91.7 10.5 %collective-permute-start.4 = (bf16[1,128,256]{2,1,0:T(8,128)(2,1)S(1)}, bf16[1,128,256]{2,1,0:T(8,128)(2,1)S(1)}, u32[]{:S(2)}, u32[]{:S(2)}) collective-permute-start(bf16[1,128,256]{2,1,0:T(8,128)(2,1)S(1)} %get-tuple-element.7), channel_id=1, source_target_pairs={{0,20},{4,16},{8,28},{12,24},{16,4},{20,0},{24,12},{28,8},{1,21},{... | collective-permute-start | bytes 196616 | tf_op jit(solution)/shard_map/ppermute | solution.py:29
  91.9 10.3 %collective-permute-start.5 = (bf16[1,128,256]{2,1,0:T(8,128)(2,1)S(1)}, bf16[1,128,256]{2,1,0:T(8,128)(2,1)S(1)}, u32[]{:S(2)}, u32[]{:S(2)}) collective-permute-start(bf16[1,128,256]{2,1,0:T(8,128)(2,1)S(1)} %get-tuple-element.6), channel_id=1, source_target_pairs={{0,24},{4,28},{8,16},{12,20},{16,8},{20,12},{24,0},{28,4},{1,25},{... | collective-permute-start | bytes 196616 | tf_op jit(solution)/shard_map/ppermute | solution.py:29
  95.3 7.0 %collective-permute-start.6 = (bf16[1,128,256]{2,1,0:T(8,128)(2,1)S(1)}, bf16[1,128,256]{2,1,0:T(8,128)(2,1)S(1)}, u32[]{:S(2)}, u32[]{:S(2)}) collective-permute-start(bf16[1,128,256]{2,1,0:T(8,128)(2,1)S(1)} %get-tuple-element.5), channel_id=1, source_target_pairs={{0,28},{4,24},{8,20},{12,16},{16,12},{20,8},{24,4},{28,0},{1,29},{... | collective-permute-start | bytes 196616 | tf_op jit(solution)/shard_map/ppermute | solution.py:29
Sparse Core Ops, SparseCore 0:
  35.9 34.2 all-gather.1
